TPU v7x, 512 devices: a whole 4x8x8 slice. The times are simulated.
512 devices in a mesh: rep: 32 (over y, x_lo, core), blk: 16 (over z, x_hi).
Axes of the slice: x: 4 (x_hi: 2, x_lo: 2; x = x_hi * 2 + x_lo), y: 8, z: 8, core: 2. Of those that a mesh axis runs over, the one named last changes fastest.
Arguments:
- green_samples: bfloat16 [2048, 2, 128, 128], P(('rep', 'blk')), may hold values from -0.22265625 to 0.22265625
- exchange_index_order: int32 [64, 128], P('blk'), may hold values from 0 to 127, each once within a row
- frequency_offset: int32 [64], P('blk'), may hold values from 0 to 127
Outputs:
- vertex: float32 [2, 64, 128, 128], P(None, 'blk', 'rep')
Inputs may be any that keep to these rules, and one draw needn't show every extreme that they name: Each row of exchange_index_order names every index of 0 to 127 once.
All inputs are finite; a program needn't handle non-finite values.
Results may differ from a plain program's by a relative error of at most 0.0003.
Values may be sent and summed in bfloat16 or wider, within the bound.
A program may use at most 128 MiB of HBM per device.

v0:
```python
import jax
import jax.numpy as jnp
from jax import lax
from jax.sharding import PartitionSpec as P


def body(green_samples, exchange_index_order, frequency_offset):
    tile_width = green_samples.shape[2]
    positions = jnp.arange(tile_width, dtype=jnp.int32)
    back_rows = (positions[None, :] - frequency_offset[:, None]) % tile_width
    composed_cols = jnp.take_along_axis(exchange_index_order, back_rows, axis=1)
    tile_portion = lax.all_gather(green_samples, "blk", axis=0, tiled=True)
    left = jnp.take(tile_portion, composed_cols, axis=3)
    real_part = jnp.einsum(
        "miqk,mkj->qij", left[:, 0], tile_portion[:, 0], preferred_element_type=jnp.float32
    )
    real_part = real_part - jnp.einsum(
        "miqk,mkj->qij", left[:, 1], tile_portion[:, 1], preferred_element_type=jnp.float32
    )
    imag_part = jnp.einsum(
        "miqk,mkj->qij", left[:, 0], tile_portion[:, 1], preferred_element_type=jnp.float32
    )
    imag_part = imag_part + jnp.einsum(
        "miqk,mkj->qij", left[:, 1], tile_portion[:, 0], preferred_element_type=jnp.float32
    )
    real_part, imag_part = (real_part, imag_part)
    stacked = jnp.stack([real_part, imag_part])
    return lax.psum_scatter(stacked, "rep", scatter_dimension=2, tiled=True)


def solution(mesh):
    placed = (P(("rep", "blk"), None, None, None), P("blk", None), P("blk"))
    return jax.shard_map(
        body, mesh=mesh, in_specs=placed, out_specs=P(None, "blk", "rep", None), check_vma=False
    )
```

profile of v0, /device:TPU:1, one launch (start us, length us, event | category | flops | bytes accessed | tf_op | source)
XLA Modules:
  0.0 423.5 jit_solution(18370117582879405168)
XLA Ops:
  6.5 0.0 copy-start
  6.5 0.0 all-gather.2.cloned.1.call-start
  6.5 1.7 copy.11
  8.2 0.0 all-gather.2.cloned.1.call-update
  8.2 0.0 all-reduce.3.cloned.1.call-start
  8.3 0.7 or_bitcast_fusion
  9.0 0.0 copy-done
  9.0 4.7 %gather_fusion.1 = s32[512]{0:T(512)S(1)} fusion(s32[4,128]{1,0:T(4,128)S(1)} %copy-done, s32[512]{0:T(512)S(1)} %or_bitcast_fusion), kind=kCustom, calls=%fused_computation.1 | custom fusion | bytes 8192 | tf_op jit(solution)/shard_map/jit(take_along_axis)/gather | solution.py:11
  13.7 0.7 fusion.14
  14.5 0.7 compare_and_fusion
  15.2 103.3 %all-gather.2.cloned.1.call-done = bf16[64,2,128,128]{3,2,0,1:T(8,128)(2,1)} async-done(((bf16[4,2,128,128]{3,2,0,1:T(8,128)(2,1)}), bf16[64,2,128,128]{3,2,0,1:T(8,128)(2,1)}) %all-gather.2.cloned.1.call-update) | async-done | bytes 4194320 | tf_op jit(solution)/shard_map/all_gather | solution.py:12
  118.5 6.6 %copy.12 = bf16[64,2,128,128]{2,0,1,3:T(8,128)(2,1)} copy(bf16[64,2,128,128]{3,2,0,1:T(8,128)(2,1)} %all-gather.2.cloned.1.call-done) | data formatting | bytes 8388608 | tf_op jit(solution)/shard_map/all_gather | solution.py:12
  125.1 16.1 %gather_fusion = bf16[512,64,2,128]{3,1,2,0:T(8,128)(2,1)} fusion(bf16[64,2,128,128]{2,0,1,3:T(8,128)(2,1)} %copy.12, s32[1024]{0:T(1024)S(1)} %pad_clamp_fusion), kind=kCustom, calls=%fused_computation | custom fusion | bytes 33556480 | tf_op jit(solution)/shard_map/jit(_take)/gather | solution.py:13
  141.1 23.1 %copy.13 = bf16[4,128,64,2,128]{1,4,2,0,3:T(8,128)(2,1)} copy(bf16[4,128,64,2,128]{4,2,3,1,0:T(8,128)(2,1)} %bitcast.98) | data formatting | bytes 33554432 | tf_op jit(solution)/shard_map/jit(_take)/gather | solution.py:13
  164.3 0.0 copy-start.1
  164.3 8.5 %select_bitcast_fusion = bf16[64,2,128,4,128]{4,2,0,3,1:T(8,128)(2,1)S(1)} fusion(bf16[4,128,64,2,128]{1,4,2,0,3:T(8,128)(2,1)} %copy.13, pred[4,128]{1,0:T(4,128)(4,1)S(1)} %compare_and_fusion), kind=kLoop, calls=%fused_computation.2 | loop fusion | flops 8388608 | bytes 33554944 | tf_op jit(solution)/shard_map/jit(_take)/select_n | solution.py:13
  172.8 0.0 copy-done.1
  172.8 2.3 fusion.5
  175.1 2.3 fusion.4
  177.5 2.3 fusion.9
  179.8 2.3 fusion.11
  182.1 0.8 pad_maximum_fusion
  183.0 0.0 all-reduce.3.cloned.1.call-update
  183.0 1.3 dynamic-slice
  184.9 230.4 %all-reduce.3.cloned.1.call-done = f32[2,4,128,128]{3,2,1,0:T(8,128)} async-done(((f32[2,4,128,128]{3,2,1,0:T(8,128)}), f32[2,4,128,128]{3,2,1,0:T(8,128)}) %all-reduce.3.cloned.1.call-update) | async-done | bytes 524304
  415.3 1.4 constant_dynamic-slice_fusion
  (1 shorter events, 0.0 us)
Async XLA Ops:
  6.5 2.5 copy-start
  6.5 112.0 %all-gather.2.cloned.1.call-start = ((), (), s32[]{:S(2)}) async-start(), calls=%async_computation | async-start | bytes 4456448 | tf_op jit(solution)/shard_map/all_gather | solution.py:12
  8.2 407.1 %all-reduce.3.cloned.1.call-start = ((), (), s32[]{:S(2)}) async-start(), calls=%async_computation.1 | async-start | bytes 1048576
  164.3 8.5 %copy-start.1 = (bf16[64,2,128,128]{3,2,0,1:T(8,128)(2,1)S(1)}, bf16[64,2,128,128]{3,2,0,1:T(8,128)(2,1)}, u32[]{:S(2)}) copy-start(bf16[64,2,128,128]{3,2,0,1:T(8,128)(2,1)} %all-gather.2.cloned.1.call-done) | copy-start | bytes 12582916
Sparse Core Ops, SparseCore 0:
  10.5 107.9 all-gather.1
  183.1 232.1 all-reduce.2
where the time goes:
time: 424 us
  waiting for transfers between devices  334 us (79%)
  local copies, waits for them, and re-layouts  54.8 us (13%)
  between operations  14.1 us (3%)
  other arithmetic  11.6 us (3%)
  matrix products  9.32 us (2%)
    unnamed x3, waiting for transfers between devices  230 us
    all_gather x1, waiting for transfers between devices, body(): tile_portion = lax.all_gather(green_samples, 'blk', axis=0, tiled=True)  103 us
    gather x2, local copies, waits for them, and re-layouts, body(): left = jnp.take(tile_portion, composed_cols, axis=3)  39.2 us
    select_n x2, other arithmetic, body(): left = jnp.take(tile_portion, composed_cols, axis=3)  9.24 us
  transfers between devices with their start and end apart: 2, of which 2 were waited for; matrix products, arithmetic and copies ran while one was open for 2% of the time, Pallas kernels for 0%

commit v1 on v0

v1 whole, which is shorter than its diff:
```python
import functools

import jax
import jax.numpy as jnp
from jax import lax
from jax.experimental import pallas as pl
from jax.experimental.pallas import tpu as pltpu
from jax.sharding import PartitionSpec as P

MESH = pl.DeviceIdType.MESH
N = 128
OWN = 4
TILES = 32
ROWS = 16
CUBE = [(1, 0, 0), (0, 1, 0), (0, 0, 1), (1, 1, 0), (1, 0, 1), (0, 1, 1), (1, 1, 1)]
PEERS = [
    (a, b, c) for c in (4, 2, 6, 0) for b in (4, 2, 6, 0) for a in (2, 0) if a or b or c
]
INDEX_PEERS = [(a, c) for c in (4, 2, 6, 0) for a in (2, 0) if a or c]


def coords():
    rep, blk = lax.axis_index("rep"), lax.axis_index("blk")
    return (blk % 2) * 2 + (rep // 2) % 2, rep // 4, blk // 2, rep % 2


def device(x, y, z, core):
    x, y, z = (x + 8) % 4, (y + 16) % 8, (z + 16) % 8
    return {"rep": (y * 2 + x % 2) * 2 + core, "blk": z * 2 + x // 2}


def remote(src, dst, send, recv, to):
    return pltpu.make_async_remote_copy(
        src_ref=src, dst_ref=dst, send_sem=send, recv_sem=recv, device_id=to, device_id_type=MESH
    )


def kernel(
    green, order, offset, out, held, cols, select, rows, left, right, total, mine, theirs,
    own_sem, send_sem, recv_sem, pass_send, pass_recv, cols_send, cols_recv, sum_send, sum_recv,
):
    x, y, z, core = coords()
    sign = 1 - 2 * core
    partner = device(x, y, z, 1 - core)
    slot = (z // 2) * 2 + x // 2

    own = pltpu.make_async_copy(green, held.at[core, 0], own_sem)
    own.start()

    barrier = pltpu.get_barrier_semaphore()
    count = 0
    for d in CUBE:
        for s in (1, -1):
            pl.semaphore_signal(
                barrier, inc=1, device_id=device(x + s * d[0], y + s * d[1], z + s * d[2], core), device_id_type=MESH
            )
            count += 1
    pl.semaphore_signal(barrier, inc=1, device_id=partner, device_id_type=MESH)
    count += 1
    for d in PEERS:
        pl.semaphore_signal(
            barrier, inc=1, device_id=device(x + d[0], y + d[1], z + d[2], core), device_id_type=MESH
        )
        count += 1

    row = lax.broadcasted_iota(jnp.int32, (8, N), 0)
    lane = lax.broadcasted_iota(jnp.int32, (8, N), 1)
    shift = jnp.zeros((8, N), jnp.int32)
    for i in range(4):
        shift = jnp.where(row == i, offset[i], shift)
    orders = jnp.concatenate([order[...], order[...]], axis=0)
    cols[slot] = jnp.take_along_axis(orders, (lane - shift + N) & (N - 1), axis=1, mode="promise_in_bounds")

    own.wait()
    pl.semaphore_wait(barrier, count)

    col_copies = []
    for i, d in enumerate(INDEX_PEERS):
        copy = remote(
            cols.at[slot], cols.at[slot], cols_send.at[i], cols_recv.at[i], device(x + d[0], y, z + d[1], core)
        )
        copy.start()
        col_copies.append(copy)
    for i, d in enumerate(CUBE):
        remote(
            held.at[core, 0], held.at[core, 1 + i], send_sem.at[1 + i], recv_sem.at[1 + i],
            device(x + sign * d[0], y + sign * d[1], z + sign * d[2], core),
        ).start()

    def arrival(o):
        return remote(held.at[core, 0], held.at[core, o], send_sem.at[o], recv_sem.at[o], partner)

    def passing(o):
        return remote(held.at[core, o], held.at[core, o], pass_send.at[o], pass_recv.at[o], partner)

    passing(0).start()
    total[...] = jnp.zeros_like(total)
    for i, d in enumerate(INDEX_PEERS):
        from_slot = ((z + 16 - d[1]) % 8 // 2) * 2 + (x + 8 - d[0]) % 4 // 2
        remote(cols.at[slot], cols.at[from_slot], cols_send.at[i], cols_recv.at[i], partner).wait_recv()
    place = lax.broadcasted_iota(jnp.int32, (N, N), 0)
    for t in range(TILES):
        wanted = cols[t // 4, t % 4 : t % 4 + 1, :]
        select[:, t * N : (t + 1) * N] = jnp.where(place == wanted, 1.0, 0.0).astype(jnp.bfloat16)

    upper = lax.broadcasted_iota(jnp.int32, (8, N), 0) < 4
    second_half = core == 1

    def class_rows(ref):
        parts = []
        for yh in range(4):
            both = ref[pl.ds(pl.multiple_of(32 * yh + 16 * (y % 2), 16), 16), :].astype(jnp.float32)
            parts.append(jnp.where(x % 2 == 0, both[0:8], both[8:16]))
        pairs = []
        for a, b in ((0, 1), (2, 3)):
            first = jnp.where(second_half, pltpu.roll(parts[a], 4, 0), parts[a])
            second = jnp.where(second_half, parts[b], pltpu.roll(parts[b], 4, 0))
            pairs.append(jnp.where(upper, first, second))
        return jnp.concatenate(pairs, axis=0).astype(jnp.bfloat16)

    def step(o, carry):
        @pl.when(o < 7)
        def _():
            arrival(o + 1).wait_recv()
            passing(o + 1).start()

        remote(held.at[core, 0], held.at[1 - core, o], pass_send.at[o], pass_recv.at[o], partner).wait_recv()
        for h in range(2):
            for m in range(OWN):
                a = h * OWN + m
                gr, gi = held[h, o, m, 0], held[h, o, m, 1]
                right[a * 256 : a * 256 + 128, 0:128] = gr
                right[a * 256 : a * 256 + 128, 128:256] = gi
                right[a * 256 + 128 : a * 256 + 256, 0:128] = -gi
                right[a * 256 + 128 : a * 256 + 256, 128:256] = gr
                for c in range(2):
                    r = (a * 2 + c) * ROWS
                    rows[r : r + ROWS, :] = class_rows(held.at[h, o, m, c])
        for t2 in range(TILES // 2):
            picked = jnp.dot(
                rows[...], select[:, t2 * 256 : (t2 + 1) * 256], preferred_element_type=jnp.float32
            ).astype(jnp.bfloat16)
            for u in range(2):
                t = t2 * 2 + u
                for b in range(4 * OWN):
                    left[t * ROWS : (t + 1) * ROWS, b * N : (b + 1) * N] = picked[
                        b * ROWS : (b + 1) * ROWS, u * N : (u + 1) * N
                    ]
        total[...] += jnp.dot(left[...], right[...], preferred_element_type=jnp.float32)
        return carry

    lax.fori_loop(0, 8, step, 0)

    for group in range(8):
        for ti in range(4):
            t = group * 4 + ti
            for yh in range(4):
                r = t * ROWS + 8 * (yh // 2)
                re, im = total[r : r + 8, 0:N], total[r : r + 8, N : 2 * N]
                if yh % 2:
                    re = pltpu.roll(re, 4, 0)
                else:
                    im = pltpu.roll(im, 4, 0)
                mine[group * 4 + yh, ti] = jnp.where(upper, re, im)

    def address(d):
        return (((z + d[2]) % 8 // 2) * 2 + (x + d[0]) % 4 // 2) * 4 + (y + d[1]) % 8 // 2

    sums = []
    for i, d in enumerate(PEERS):
        copy = remote(
            mine.at[address(d)], theirs.at[i], sum_send.at[i], sum_recv.at[i],
            device(x + d[0], y + d[1], z + d[2], core),
        )
        copy.start()
        sums.append(copy)
    acc = mine[address((0, 0, 0))]
    for i, copy in reversed(list(enumerate(sums))):
        copy.wait_recv()
        acc = acc + theirs[i]
    out[...] = acc

    for copy in sums + col_copies:
        copy.wait_send()

    def drain(o, carry):
        passing(o).wait_send()

        @pl.when(o > 0)
        def _():
            arrival(o).wait_send()

        return carry

    lax.fori_loop(0, 8, drain, 0)


def body(green_samples, exchange_index_order, frequency_offset):
    bf16, f32 = jnp.bfloat16, jnp.float32
    dma = pltpu.SemaphoreType.DMA
    summed = pl.pallas_call(
        kernel,
        out_shape=jax.ShapeDtypeStruct((4, 8, N), f32),
        in_specs=[
            pl.BlockSpec(memory_space=pl.ANY),
            pl.BlockSpec(memory_space=pltpu.VMEM),
            pl.BlockSpec(memory_space=pltpu.SMEM),
        ],
        out_specs=pl.BlockSpec(memory_space=pltpu.VMEM),
        scratch_shapes=[
            pltpu.VMEM((2, 8, OWN, 2, N, N), bf16),
            pltpu.VMEM((8, 8, N), jnp.int32),
            pltpu.VMEM((N, TILES * N), bf16),
            pltpu.VMEM((4 * OWN * ROWS, N), bf16),
            pltpu.VMEM((TILES * ROWS, 4 * OWN * N), bf16),
            pltpu.VMEM((4 * OWN * N, 2 * N), bf16),
            pltpu.VMEM((TILES * ROWS, 2 * N), f32),
            pltpu.VMEM((32, 4, 8, N), f32),
            pltpu.VMEM((31, 4, 8, N), f32),
            dma, dma((8,)), dma((8,)), dma((8,)), dma((8,)), dma((7,)), dma((7,)), dma((31,)), dma((31,)),
        ],
        compiler_params=pltpu.CompilerParams(collective_id=0, has_side_effects=True, vmem_limit_bytes=48 << 20),
        name="vertex",
    )(green_samples, exchange_index_order, frequency_offset)
    return summed.reshape(4, 2, 4, N).transpose(1, 0, 2, 3)


def solution(mesh):
    placed = (P(("rep", "blk"), None, None, None), P("blk", None), P("blk"))
    return jax.shard_map(
        body, mesh=mesh, in_specs=placed, out_specs=P(None, "blk", "rep", None), check_vma=False
    )
```

time: 424 us -> 61 us (0.14)
  the two profiles are of different devices: /device:TPU:1 before, /device:TPU:8 now
where the time goes in v1:
time: 61 us; the launch traced here: 60.9 us
  Pallas kernels  58 us (95%)
  local copies, waits for them, and re-layouts  2.89 us (5%)
    pallas_call x1, Pallas kernels, body(): pl.pallas_call(kernel, out_shape=jax.ShapeDtypeStruct((4, 8, N), f32), in...  58 us
    unnamed x6, local copies, waits for them, and re-layouts  2.29 us

profile of v1, /device:TPU:8, one launch (start us, length us, event | category | flops | bytes accessed | tf_op | source)
XLA Modules:
  0.0 60.9 jit_solution(17210446843871264601)
XLA Ops:
  0.0 0.0 copy-start
  0.0 0.9 %copy-done = bf16[4,2,128,128]{3,2,1,0:T(8,128)(2,1)S(1)} copy-done((bf16[4,2,128,128]{3,2,1,0:T(8,128)(2,1)S(1)}, bf16[4,2,128,128]{3,2,1,0:T(8,128)(2,1)}, u32[]{:S(2)}) %copy-start) | copy-done | bytes 262168
  1.0 0.0 copy-start.1
  1.0 0.7 %copy-done.1 = s32[4,128]{1,0:T(4,128)S(1)} copy-done((s32[4,128]{1,0:T(4,128)S(1)}, s32[4,128]{1,0:T(4,128)}, u32[]{:S(2)}) %copy-start.1) | copy-done | bytes 2072
  1.6 0.0 copy-start.2
  1.6 0.7 %copy-done.2 = s32[4]{0:T(128)S(1)} copy-done((s32[4]{0:T(128)S(1)}, s32[4]{0:T(128)}, u32[]{:S(2)}) %copy-start.2) | copy-done | bytes 40
  2.3 58.0 %vertex.1 = f32[4,8,128]{2,1,0:T(8,128)S(1)} custom-call(bf16[4,2,128,128]{3,2,1,0:T(8,128)(2,1)S(1)} %copy-done, s32[4,128]{1,0:T(4,128)S(1)} %copy-done.1, s32[4]{0:T(128)S(1)} %copy-done.2), custom_call_target="tpu_custom_call" | custom-call | tf_op jit(solution)/shard_map/vertex/pallas_call | solution.py:201
  60.2 0.6 %copy.6 = f32[4,2,4,128]{3,2,0,1:T(4,128)} copy(f32[4,2,4,128]{3,2,1,0:T(4,128)S(1)} %bitcast.4) | data formatting | bytes 32768 | tf_op jit(solution)/shard_map/reshape | solution.py:225
Async XLA Ops:
  0.0 0.9 %copy-start = (bf16[4,2,128,128]{3,2,1,0:T(8,128)(2,1)S(1)}, bf16[4,2,128,128]{3,2,1,0:T(8,128)(2,1)}, u32[]{:S(2)}) copy-start(bf16[4,2,128,128]{3,2,1,0:T(8,128)(2,1)} %green.1) | copy-start | bytes 786436
  1.0 0.7 %copy-start.1 = (s32[4,128]{1,0:T(4,128)S(1)}, s32[4,128]{1,0:T(4,128)}, u32[]{:S(2)}) copy-start(s32[4,128]{1,0:T(4,128)} %order.1) | copy-start | bytes 6148
  1.6 0.7 %copy-start.2 = (s32[4]{0:T(128)S(1)}, s32[4]{0:T(128)}, u32[]{:S(2)}) copy-start(s32[4]{0:T(128)} %offset.1) | copy-start | bytes 52

commit v2 on v0

v2 whole, which is shorter than its diff:
```python
import jax
import jax.numpy as jnp
from jax import lax
from jax.experimental import pallas as pl
from jax.experimental.pallas import tpu as pltpu
from jax.sharding import PartitionSpec as P

MESH = pl.DeviceIdType.MESH
N = 128
OWN = 4
CHUNK = 2 * OWN
ROWS = 16
CORNERS = [(), (0,), (1,), (2,), (0, 1), (0, 2), (1, 2), (0, 1, 2)]
ORDERS = [(0, 1, 2), (1, 2, 0), (2, 0, 1), (0, 1, 2), (1, 2, 0)]
PIECES = range(len(ORDERS))


def corner(*axes):
    return CORNERS.index(tuple(sorted(axes)))


def coords():
    rep, blk = lax.axis_index("rep"), lax.axis_index("blk")
    return (blk % 2) * 2 + (rep // 2) % 2, rep // 4, blk // 2, rep % 2


def device(x, y, z, core):
    x, y, z = (x + 8) % 4, (y + 16) % 8, (z + 16) % 8
    return {"rep": (y * 2 + x % 2) * 2 + core, "blk": z * 2 + x // 2}


def remote(src, dst, send, recv, to):
    return pltpu.make_async_remote_copy(
        src_ref=src, dst_ref=dst, send_sem=send, recv_sem=recv, device_id=to, device_id_type=MESH
    )


def signal(sem, to):
    pl.semaphore_signal(sem, inc=1, device_id=to, device_id_type=MESH)


def kernel(
    green, order, offset, out,
    held, orders, shifts, cols, select, rows, left, total, mine, theirs,
    own_sem, send_sem, recv_sem, pass_send, pass_recv, cols_send, cols_recv, sum_send, sum_recv, known,
):
    x, y, z, core = coords()
    sign = 1 - 2 * core
    partner = device(x, y, z, 1 - core)
    across = 3 - x

    small = [
        pltpu.make_async_copy(order, orders.at[pl.ds(0, 4)], own_sem.at[2]),
        pltpu.make_async_copy(order, orders.at[pl.ds(4, 4)], own_sem.at[3]),
        pltpu.make_async_copy(offset, shifts, own_sem.at[4]),
    ]
    own = [
        pltpu.make_async_copy(green.at[:, c], held.at[0, core, :, :, pl.ds(c * N, N)], own_sem.at[c])
        for c in range(2)
    ]
    for copy in small + own:
        copy.start()

    barrier = pltpu.get_barrier_semaphore()
    near = [device(x + s, y, z, core) for s in (1, -1)]
    near += [device(x, y + s, z, core) for s in (1, -1)]
    near += [device(x, y, z + s, core) for s in (1, -1)]
    near += [partner, device(across, y, z, core), device(x + 2, y, z, core)]
    for s in (2, -2):
        near += [device(x, y, z + s, core), device(across, y, z + s, core), device(x, y + s, z, core)]
    for to in near:
        signal(barrier, to)

    for copy in small:
        copy.wait()
    row = lax.broadcasted_iota(jnp.int32, (8, N), 0)
    lane = lax.broadcasted_iota(jnp.int32, (8, N), 1)
    shift = jnp.zeros((8, N), jnp.int32)
    for i in range(4):
        shift = jnp.where(row == i, shifts[i], shift)
    cols[0, 0] = jnp.take_along_axis(orders[...], (lane - shift + N) & (N - 1), axis=1, mode="promise_in_bounds")

    for copy in own:
        copy.wait()
    pl.semaphore_wait(barrier, len(near))

    def send_cols(i, src, dst, to):
        return remote(cols.at[src[0], src[1]], cols.at[dst[0], dst[1]], cols_send.at[i], cols_recv.at[i], to)

    col_copies = [
        send_cols(0, (0, 0), (0, 1), device(across, y, z, core)),
        send_cols(1, (0, 0), (3, 0), device(x, y, z + 2, core)),
        send_cols(2, (0, 0), (1, 0), device(x, y, z - 2, core)),
        send_cols(3, (0, 0), (3, 1), device(across, y, z + 2, core)),
        send_cols(4, (0, 0), (1, 1), device(across, y, z - 2, core)),
        send_cols(5, (1, 0), (2, 0), device(x, y, z - 2, core)),
        send_cols(6, (3, 1), (2, 1), device(x, y, z + 2, core)),
    ]
    for copy in col_copies[:5]:
        copy.start()
    onward = [device(x + sign, y, z, core), device(x, y + sign, z, core), device(x, y, z + sign, core)]

    def piece(o, p):
        if p < 3:
            return held.at[o, core, p]
        return held.at[o, core, 3, :, pl.ds((p - 3) * N, N)]

    def hop(p, *ranks):
        axes = [ORDERS[p][r] for r in ranks]
        o = corner(*axes)
        return remote(
            piece(corner(*axes[:-1]), p), piece(o, p), send_sem.at[o, p], recv_sem.at[o, p], onward[axes[-1]]
        )

    for r in range(3):
        for p in PIECES:
            hop(p, r).start()

    def passing(o):
        return remote(held.at[o, core], held.at[o, core], pass_send.at[o], pass_recv.at[o], partner)

    def passed(o):
        remote(held.at[o, core], held.at[o, 1 - core], pass_send.at[o], pass_recv.at[o], partner).wait_recv()

    passing(0).start()
    for s in (2, -2):
        signal(known.at[0], device(x, y + s, z, core))
    total[...] = jnp.zeros_like(total)
    place = lax.broadcasted_iota(jnp.int32, (N, N), 0)
    upper = row < 4
    second_half = core == 1

    def class_rows(o, h, m, c):
        parts = []
        for b in range(4):
            start = pl.multiple_of(32 * ((y // 2 + b) % 4) + 16 * (y % 2), 16)
            both = held[o, h, m, pl.ds(start, 16), c * N : (c + 1) * N].astype(jnp.float32)
            parts.append(jnp.where(x % 2 == 0, both[0:8], both[8:16]))
        pairs = []
        for a, b in ((0, 1), (2, 3)):
            first = jnp.where(second_half, pltpu.roll(parts[a], 4, 0), parts[a])
            second = jnp.where(second_half, parts[b], pltpu.roll(parts[b], 4, 0))
            pairs.append(jnp.where(upper, first, second))
        return jnp.concatenate(pairs, axis=0).astype(jnp.bfloat16)

    def take_rows(o):
        for h in range(2):
            for m in range(OWN):
                for c in range(2):
                    r = ((h * OWN + m) * 2 + c) * ROWS
                    rows[r : r + ROWS, :] = class_rows(o, h, m, c)

    def choose(g):
        for t in range(8):
            wanted = cols[g, t // 4, t % 4 : t % 4 + 1, :]
            select[g, :, t * N : (t + 1) * N] = jnp.where(place == wanted, 1.0, 0.0).astype(jnp.bfloat16)

    def unit(g, o):
        buf = left.at[g % 2]
        for t2 in range(4):
            picked = jnp.dot(
                rows[...], select[g, :, t2 * 256 : (t2 + 1) * 256], preferred_element_type=jnp.float32
            ).astype(jnp.bfloat16)
            for u in range(2):
                t = t2 * 2 + u
                for a in range(CHUNK):
                    for c in range(2):
                        r = (a * 2 + c) * ROWS
                        buf[c * N + t * ROWS : c * N + (t + 1) * ROWS, a * N : (a + 1) * N] = picked[
                            r : r + ROWS, u * N : (u + 1) * N
                        ]
        total[g] += jnp.dot(
            buf[...], held[o].reshape(CHUNK * N, 2 * N), preferred_element_type=jnp.float32
        )

    passed(0)
    take_rows(0)
    col_copies[0].wait_recv()
    choose(0)
    unit(0, 0)
    for p in PIECES:
        hop(p, 0).wait_recv()
        hop(p, 0, 1).start()
        hop(p, 0, 2).start()
    col_copies[2].wait_recv()
    col_copies[5].start()
    col_copies[3].wait_recv()
    col_copies[6].start()
    col_copies[1].wait_recv()
    col_copies[4].wait_recv()
    choose(1)
    unit(1, 0)
    for p in PIECES:
        hop(p, 1).wait_recv()
        hop(p, 1, 2).start()
    choose(3)
    unit(3, 0)
    for p in PIECES:
        hop(p, 2).wait_recv()
    for o in (1, 2, 3):
        passing(o).start()
    pl.semaphore_wait(known.at[0], 2)
    signal(known.at[1], device(x + 2, y, z, core))
    col_copies[5].wait_recv()
    col_copies[6].wait_recv()
    choose(2)
    unit(2, 0)
    for p in PIECES:
        hop(p, 0, 1).wait_recv()
        hop(p, 0, 1, 2).start()

    def step(o, carry):
        passed(o)
        take_rows(o)
        for g in range(4):
            unit(g, o)

        @pl.when(o == 1)
        def _():
            for p in PIECES:
                hop(p, 0, 2).wait_recv()
                hop(p, 1, 2).wait_recv()
            for i in (4, 5, 6):
                passing(i).start()

        @pl.when(o == 3)
        def _():
            for p in PIECES:
                hop(p, 0, 1, 2).wait_recv()
            passing(7).start()

        @pl.when(o == 2)
        def _():
            pl.semaphore_wait(known.at[1], 1)
            for s in (2, -2):
                signal(known.at[2], device(x, y, z + s, core))

        @pl.when(o == 4)
        def _():
            pl.semaphore_wait(known.at[2], 2)
            for s in (2, -2):
                signal(known.at[3], device(x, y, z + s, core))

        return carry

    lax.fori_loop(1, 7, step, 0)

    passed(7)
    take_rows(7)
    pl.semaphore_wait(known.at[3], 2)
    sums = []
    for g in (2, 1, 3, 0):
        unit(g, 7)
        for e in range(2):
            for ti in range(4):
                for half in range(2):
                    r = (e * 4 + ti) * ROWS + 8 * half
                    re = total[g, r : r + 8, 0:N] - total[g, N + r : N + r + 8, N : 2 * N]
                    im = total[g, r : r + 8, N : 2 * N] + total[g, N + r : N + r + 8, 0:N]
                    mine[g, e, 2 * half, ti] = jnp.where(upper, re, pltpu.roll(im, 4, 0))
                    mine[g, e, 2 * half + 1, ti] = jnp.where(upper, pltpu.roll(re, 4, 0), im)
            for b in (2, 1, 3, 0):
                if g or e or b:
                    copy = remote(
                        mine.at[g, e, b], theirs.at[g, e, b], sum_send.at[g, e, b], sum_recv.at[g, e, b],
                        device(x + 2 * e, y + 2 * b, z + 2 * g, core),
                    )
                    copy.start()
                    sums.append(((g, e, b), copy))
    acc = mine[0, 0, 0]
    for place_of, copy in reversed(sums):
        copy.wait_recv()
        acc = acc + theirs[place_of]
    out[...] = acc

    for _, copy in sums:
        copy.wait_send()
    for copy in col_copies:
        copy.wait_send()

    for o in range(8):
        passing(o).wait_send()
    for p in PIECES:
        for ranks in ((0,), (1,), (2,), (0, 1), (0, 2), (1, 2), (0, 1, 2)):
            hop(p, *ranks).wait_send()


def body(green_samples, exchange_index_order, frequency_offset):
    bf16, f32, i32 = jnp.bfloat16, jnp.float32, jnp.int32
    dma, regular = pltpu.SemaphoreType.DMA, pltpu.SemaphoreType.REGULAR
    summed = pl.pallas_call(
        kernel,
        out_shape=jax.ShapeDtypeStruct((4, 8, N), f32),
        in_specs=[pl.BlockSpec(memory_space=pltpu.HBM)] * 3,
        out_specs=pl.BlockSpec(memory_space=pltpu.VMEM),
        scratch_shapes=[
            pltpu.VMEM((8, 2, OWN, N, 2 * N), bf16),
            pltpu.VMEM((8, N), i32),
            pltpu.SMEM((4,), i32),
            pltpu.VMEM((4, 2, 8, N), i32),
            pltpu.VMEM((4, N, 8 * N), bf16),
            pltpu.VMEM((CHUNK * 2 * ROWS, N), bf16),
            pltpu.VMEM((2, 2 * N, CHUNK * N), bf16),
            pltpu.VMEM((4, 2 * N, 2 * N), f32),
            pltpu.VMEM((4, 2, 4, 4, 8, N), f32),
            pltpu.VMEM((4, 2, 4, 4, 8, N), f32),
            dma((5,)), dma((8, 5)), dma((8, 5)), dma((8,)), dma((8,)), dma((7,)), dma((7,)),
            dma((4, 2, 4)), dma((4, 2, 4)), regular((4,)),
        ],
        compiler_params=pltpu.CompilerParams(collective_id=0, has_side_effects=True, vmem_limit_bytes=67043328),
        name="vertex",
    )(green_samples, exchange_index_order, frequency_offset)
    return summed.reshape(4, 2, 4, N).transpose(1, 0, 2, 3)


def solution(mesh):
    placed = (P(("rep", "blk"), None, None, None), P("blk", None), P("blk"))
    return jax.shard_map(
        body, mesh=mesh, in_specs=placed, out_specs=P(None, "blk", "rep", None), check_vma=False
    )
```

time: 424 us -> 52.4 us (0.12)
  waiting for transfers between devices: 334 us -> 0 us
  local copies, waits for them, and re-layouts: 54.8 us -> 1.33 us
  Pallas kernels: 0 us -> 50.8 us
  between operations: 14.1 us -> 0.01 us
  other arithmetic: 11.6 us -> 0 us
  matrix products: 9.32 us -> 0 us
    unnamed x3 -> x0, waiting for transfers between devices: 230 us -> none
    all_gather x1 -> x0, waiting for transfers between devices: 103 us -> none  [body(): tile_portion = lax.all_gather(green_samples, 'blk', axis=0, tiled=True)]
    pallas_call x0 -> x1, Pallas kernels: none -> 50.8 us  [body(): pl.pallas_call(kernel, out_shape=jax.ShapeDtypeStruct((4, 8, N), f32), in...]
    gather x3 -> x0, local copies, waits for them, and re-layouts: 43.9 us -> none  [the longest x2 39.2 us: body(): left = jnp.take(tile_portion, composed_cols, axis=3)]
    dot_general x4 -> x0, matrix products: 9.32 us -> none  [the longest x1 2.35 us: body(): jnp.einsum('miqk,mkj->qij', left[:, 0], tile_portion[:, 1], preferred_ele...]
    select_n x2 -> x0, other arithmetic: 9.24 us -> none  [body(): left = jnp.take(tile_portion, composed_cols, axis=3)]
    all_gather x1 -> x0, local copies, waits for them, and re-layouts: 6.56 us -> none  [body(): tile_portion = lax.all_gather(green_samples, 'blk', axis=0, tiled=True)]
    unnamed x7 -> x0, local copies, waits for them, and re-layouts: 4.32 us -> none
  transfers between devices with their start and end apart: 2 -> 0, of which waited for: 2 -> 0; matrix products, arithmetic and copies ran while one was open for 2% -> 0% of each run, Pallas kernels for 0% -> 0%
where the time goes in v2:
time: 52.4 us; the launch traced here: 52.1 us
  Pallas kernels  50.8 us (97%)
  local copies, waits for them, and re-layouts  1.33 us (3%)
    pallas_call x1, Pallas kernels, body(): pl.pallas_call(kernel, out_shape=jax.ShapeDtypeStruct((4, 8, N), f32), in...  50.8 us
    reshape x1, local copies, waits for them, and re-layouts, body(): return summed.reshape(4, 2, 4, N).transpose(1, 0, 2, 3)  1.33 us

profile of v2, /device:TPU:1, one launch (start us, length us, event | category | flops | bytes accessed | tf_op | source)
XLA Modules:
  0.0 52.1 jit_solution(6754252783693927589)
XLA Ops:
  0.0 50.8 %vertex.1 = f32[4,8,128]{2,1,0:T(8,128)} custom-call(bf16[4,2,128,128]{3,2,1,0:T(8,128)(2,1)} %green.1, s32[4,128]{1,0:T(4,128)} %order.1, s32[4]{0:T(128)} %offset.1), custom_call_target="tpu_custom_call" | custom-call | tf_op jit(solution)/shard_map/vertex/pallas_call | solution.py:291
  50.8 1.3 %copy.6 = f32[4,2,4,128]{3,2,0,1:T(4,128)} copy(f32[4,2,4,128]{3,2,1,0:T(4,128)} %bitcast.4) | data formatting | bytes 32768 | tf_op jit(solution)/shard_map/reshape | solution.py:313

commit v3 on v2

--- a/solution.py
+++ b/solution.py
@@ -10,6 +10,7 @@
 OWN = 4
 CHUNK = 2 * OWN
 ROWS = 16
+LEVELS = 32766.0
 CORNERS = [(), (0,), (1,), (2,), (0, 1), (0, 2), (1, 2), (0, 1, 2)]
 ORDERS = [(0, 1, 2), (1, 2, 0), (2, 0, 1), (0, 1, 2), (1, 2, 0)]
 PIECES = range(len(ORDERS))
@@ -37,6 +38,31 @@
 
 def signal(sem, to):
     pl.semaphore_signal(sem, inc=1, device_id=to, device_id_type=MESH)
+
+
+def pack(parts, ref, at):
+    most = jnp.maximum(
+        jnp.maximum(jnp.abs(parts[0]), jnp.abs(parts[1])), jnp.maximum(jnp.abs(parts[2]), jnp.abs(parts[3]))
+    )
+    most = jnp.max(most, axis=0, keepdims=True)
+    power = jnp.clip(jnp.ceil(jnp.log2(most) + 1e-3), -111.0, 110.0)
+    fit = jnp.exp2(-power) * LEVELS
+    whole = [jnp.floor(v * fit + 0.5).astype(jnp.int32) for v in parts]
+    for i in range(2):
+        ref[(*at, slice(8 * i, 8 * i + 8))] = jnp.bitwise_or(
+            jnp.left_shift(whole[2 * i], 16), jnp.bitwise_and(whole[2 * i + 1], 0xFFFF)
+        )
+    ref[(*at, slice(16, 17))] = power.astype(jnp.int32)
+
+
+def unpack(ref, at):
+    step = jnp.exp2(ref[(*at, slice(16, 17))].astype(jnp.float32)) * (1.0 / LEVELS)
+    parts = []
+    for i in range(2):
+        words = ref[(*at, slice(8 * i, 8 * i + 8))]
+        for whole in (jnp.right_shift(words, 16), jnp.right_shift(jnp.left_shift(words, 16), 16)):
+            parts.append(whole.astype(jnp.float32) * step)
+    return parts
 
 
 def kernel(
@@ -65,9 +91,8 @@
     near = [device(x + s, y, z, core) for s in (1, -1)]
     near += [device(x, y + s, z, core) for s in (1, -1)]
     near += [device(x, y, z + s, core) for s in (1, -1)]
-    near += [partner, device(across, y, z, core), device(x + 2, y, z, core)]
-    for s in (2, -2):
-        near += [device(x, y, z + s, core), device(across, y, z + s, core), device(x, y + s, z, core)]
+    around = list(near)
+    near += [partner]
     for to in near:
         signal(barrier, to)
 
@@ -96,14 +121,13 @@
         send_cols(5, (1, 0), (2, 0), device(x, y, z - 2, core)),
         send_cols(6, (3, 1), (2, 1), device(x, y, z + 2, core)),
     ]
-    for copy in col_copies[:5]:
-        copy.start()
+    col_copies[0].start()
     onward = [device(x + sign, y, z, core), device(x, y + sign, z, core), device(x, y, z + sign, core)]
 
-    def piece(o, p):
+    def piece(o, p, owner=core):
         if p < 3:
-            return held.at[o, core, p]
-        return held.at[o, core, 3, :, pl.ds((p - 3) * N, N)]
+            return held.at[o, owner, p]
+        return held.at[o, owner, 3, :, pl.ds((p - 3) * N, N)]
 
     def hop(p, *ranks):
         axes = [ORDERS[p][r] for r in ranks]
@@ -117,14 +141,24 @@
             hop(p, r).start()
 
     def passing(o):
-        return remote(held.at[o, core], held.at[o, core], pass_send.at[o], pass_recv.at[o], partner)
+        return remote(held.at[o, core], held.at[o, core], pass_send.at[o, 0], pass_recv.at[o, 0], partner)
 
     def passed(o):
-        remote(held.at[o, core], held.at[o, 1 - core], pass_send.at[o], pass_recv.at[o], partner).wait_recv()
+        remote(held.at[o, core], held.at[o, 1 - core], pass_send.at[o, 0], pass_recv.at[o, 0], partner).wait_recv()
+
+    def passing_last(p):
+        return remote(piece(7, p), piece(7, p), pass_send.at[7, p], pass_recv.at[7, p], partner)
 
     passing(0).start()
+    for to in around:
+        signal(known.at[4], to)
+    pl.semaphore_wait(known.at[4], 6)
+    for to in around[4:]:
+        signal(known.at[5], to)
     for s in (2, -2):
         signal(known.at[0], device(x, y + s, z, core))
+    col_copies[1].start()
+    col_copies[2].start()
     total[...] = jnp.zeros_like(total)
     place = lax.broadcasted_iota(jnp.int32, (N, N), 0)
     upper = row < 4
@@ -148,72 +182,99 @@
             for m in range(OWN):
                 for c in range(2):
                     r = ((h * OWN + m) * 2 + c) * ROWS
-                    rows[r : r + ROWS, :] = class_rows(o, h, m, c)
+                    rows[o, r : r + ROWS, :] = class_rows(o, h, m, c)
 
     def choose(g):
         for t in range(8):
             wanted = cols[g, t // 4, t % 4 : t % 4 + 1, :]
             select[g, :, t * N : (t + 1) * N] = jnp.where(place == wanted, 1.0, 0.0).astype(jnp.bfloat16)
 
-    def unit(g, o):
-        buf = left.at[g % 2]
-        for t2 in range(4):
+    order_of = [(zh + 4 - z // 2) % 4 for zh in (0, 1, 3, 2)]
+
+    def pick(g, o, k):
+        for t in range(4, 8):
+            wanted = jnp.broadcast_to(cols[g, t // 4, t % 4 : t % 4 + 1, :], (8, N))
+            for a in range(CHUNK):
+                for c in range(2):
+                    r = (a * 2 + c) * ROWS
+                    to = k * 2 * N + c * N + t * ROWS
+                    halves = [
+                        jnp.take_along_axis(rows[o, r + i : r + i + 8, :].astype(jnp.float32), wanted, axis=1, mode="promise_in_bounds")
+                        for i in (0, 8)
+                    ]
+                    left[to : to + ROWS, a * N : (a + 1) * N] = jnp.concatenate(halves, axis=0).astype(jnp.bfloat16)
+        for t2 in range(2):
             picked = jnp.dot(
-                rows[...], select[g, :, t2 * 256 : (t2 + 1) * 256], preferred_element_type=jnp.float32
+                rows[o], select[g, :, t2 * 256 : (t2 + 1) * 256], preferred_element_type=jnp.float32
             ).astype(jnp.bfloat16)
             for u in range(2):
                 t = t2 * 2 + u
                 for a in range(CHUNK):
                     for c in range(2):
                         r = (a * 2 + c) * ROWS
-                        buf[c * N + t * ROWS : c * N + (t + 1) * ROWS, a * N : (a + 1) * N] = picked[
-                            r : r + ROWS, u * N : (u + 1) * N
-                        ]
-        total[g] += jnp.dot(
-            buf[...], held[o].reshape(CHUNK * N, 2 * N), preferred_element_type=jnp.float32
+                        to = k * 2 * N + c * N + t * ROWS
+                        left[to : to + ROWS, a * N : (a + 1) * N] = picked[r : r + ROWS, u * N : (u + 1) * N]
+
+    def multiply(o, first, count, place):
+        total[pl.ds(place, count * 2 * N), :] += jnp.dot(
+            left[first * 2 * N : (first + count) * 2 * N, :],
+            held[o].reshape(CHUNK * N, 2 * N),
+            preferred_element_type=jnp.float32,
         )
 
+    def unit(g):
+        zh = (z // 2 + g) % 4
+        pick(g, 0, g)
+        multiply(0, g, 1, pl.multiple_of((zh + zh // 2 - 2 * (zh // 3)) * 2 * N, 2 * N))
+
+    def units(o, first, count):
+        for k in range(first, first + count):
+            pick(order_of[k], o, k)
+        multiply(o, first, count, first * 2 * N)
+
+    pl.semaphore_wait(known.at[5], 2)
+    col_copies[3].start()
+    col_copies[4].start()
     passed(0)
     take_rows(0)
     col_copies[0].wait_recv()
     choose(0)
-    unit(0, 0)
+    unit(0)
     for p in PIECES:
         hop(p, 0).wait_recv()
         hop(p, 0, 1).start()
         hop(p, 0, 2).start()
     col_copies[2].wait_recv()
     col_copies[5].start()
-    col_copies[3].wait_recv()
-    col_copies[6].start()
-    col_copies[1].wait_recv()
-    col_copies[4].wait_recv()
-    choose(1)
-    unit(1, 0)
     for p in PIECES:
         hop(p, 1).wait_recv()
         hop(p, 1, 2).start()
-    choose(3)
-    unit(3, 0)
     for p in PIECES:
         hop(p, 2).wait_recv()
     for o in (1, 2, 3):
         passing(o).start()
+    col_copies[1].wait_recv()
+    col_copies[3].wait_recv()
+    col_copies[6].start()
+    col_copies[4].wait_recv()
+    choose(1)
+    unit(1)
+    for p in PIECES:
+        hop(p, 0, 1).wait_recv()
+        hop(p, 0, 1, 2).start()
+    choose(3)
+    unit(3)
     pl.semaphore_wait(known.at[0], 2)
     signal(known.at[1], device(x + 2, y, z, core))
     col_copies[5].wait_recv()
     col_copies[6].wait_recv()
     choose(2)
-    unit(2, 0)
-    for p in PIECES:
-        hop(p, 0, 1).wait_recv()
-        hop(p, 0, 1, 2).start()
-
-    def step(o, carry):
+    unit(2)
+
+    def settle(o, carry):
         passed(o)
         take_rows(o)
-        for g in range(4):
-            unit(g, o)
+        units(o, 0, 4)
 
         @pl.when(o == 1)
         def _():
@@ -222,65 +283,90 @@
                 hop(p, 1, 2).wait_recv()
             for i in (4, 5, 6):
                 passing(i).start()
-
-        @pl.when(o == 3)
+            pl.semaphore_wait(known.at[1], 1)
+            for s in (2, -2):
+                signal(known.at[2], device(x, y, z + s, core))
+
+        return carry
+
+    lax.fori_loop(1, 4, settle, 0)
+    pl.semaphore_wait(known.at[2], 2)
+    for s in (2, -2):
+        signal(known.at[3], device(x, y, z + s, core))
+
+    def first_two(o, carry):
+        passed(o)
+        take_rows(o)
+        units(o, 0, 2)
+
+        @pl.when(o == 5)
         def _():
             for p in PIECES:
                 hop(p, 0, 1, 2).wait_recv()
-            passing(7).start()
-
-        @pl.when(o == 2)
-        def _():
-            pl.semaphore_wait(known.at[1], 1)
-            for s in (2, -2):
-                signal(known.at[2], device(x, y, z + s, core))
-
-        @pl.when(o == 4)
-        def _():
-            pl.semaphore_wait(known.at[2], 2)
-            for s in (2, -2):
-                signal(known.at[3], device(x, y, z + s, core))
+                passing_last(p).start()
 
         return carry
 
-    lax.fori_loop(1, 7, step, 0)
-
-    passed(7)
+    lax.fori_loop(4, 7, first_two, 0)
+    for p in PIECES:
+        far = piece(7, p, 1 - core)
+        remote(piece(7, p), far, pass_send.at[7, p], pass_recv.at[7, p], partner).wait_recv()
     take_rows(7)
     pl.semaphore_wait(known.at[3], 2)
-    sums = []
-    for g in (2, 1, 3, 0):
-        unit(g, 7)
+
+    def finish(k):
+        g, base = order_of[k], k * 2 * N
         for e in range(2):
+            parts = [[], [], [], []]
             for ti in range(4):
                 for half in range(2):
-                    r = (e * 4 + ti) * ROWS + 8 * half
-                    re = total[g, r : r + 8, 0:N] - total[g, N + r : N + r + 8, N : 2 * N]
-                    im = total[g, r : r + 8, N : 2 * N] + total[g, N + r : N + r + 8, 0:N]
-                    mine[g, e, 2 * half, ti] = jnp.where(upper, re, pltpu.roll(im, 4, 0))
-                    mine[g, e, 2 * half + 1, ti] = jnp.where(upper, pltpu.roll(re, 4, 0), im)
+                    r = base + (e * 4 + ti) * ROWS + 8 * half
+                    re = total[r : r + 8, 0:N] - total[N + r : N + r + 8, N : 2 * N]
+                    im = total[r : r + 8, N : 2 * N] + total[N + r : N + r + 8, 0:N]
+                    parts[2 * half].append(jnp.where(upper, re, pltpu.roll(im, 4, 0)))
+                    parts[2 * half + 1].append(jnp.where(upper, pltpu.roll(re, 4, 0), im))
             for b in (2, 1, 3, 0):
-                if g or e or b:
-                    copy = remote(
-                        mine.at[g, e, b], theirs.at[g, e, b], sum_send.at[g, e, b], sum_recv.at[g, e, b],
-                        device(x + 2 * e, y + 2 * b, z + 2 * g, core),
-                    )
+                pack(parts[b], mine, (g, e, b))
+                copy = summing(g, e, b)
+                if e or b:
                     copy.start()
-                    sums.append(((g, e, b), copy))
-    acc = mine[0, 0, 0]
-    for place_of, copy in reversed(sums):
-        copy.wait_recv()
-        acc = acc + theirs[place_of]
-    out[...] = acc
-
-    for _, copy in sums:
-        copy.wait_send()
+                else:
+                    pl.when(g != 0)(copy.start)
+
+    def summing(g, e, b):
+        return remote(
+            mine.at[g, e, b], theirs.at[g, e, b], sum_send.at[g, e, b], sum_recv.at[g, e, b],
+            device(x + 2 * e, y + 2 * b, z + 2 * g, core),
+        )
+
+    units(7, 0, 2)
+    finish(0)
+    finish(1)
+
+    def last_two(o, carry):
+        units(o, 2, 2)
+        return carry
+
+    lax.fori_loop(4, 8, last_two, 0)
+    finish(2)
+    finish(3)
+    kept = unpack(mine, (0, 0, 0))
+    sums = [(g, e, b) for g in range(4) for e in range(2) for b in range(4)][1:]
+    for at in sums:
+        summing(*at).wait_recv()
+        kept = [k + u for k, u in zip(kept, unpack(theirs, at))]
+    for ti in range(4):
+        out[ti] = kept[ti]
+
+    for at in sums:
+        summing(*at).wait_send()
     for copy in col_copies:
         copy.wait_send()
 
-    for o in range(8):
+    for o in range(7):
         passing(o).wait_send()
     for p in PIECES:
+        passing_last(p).wait_send()
         for ranks in ((0,), (1,), (2,), (0, 1), (0, 2), (1, 2), (0, 1, 2)):
             hop(p, *ranks).wait_send()
 
@@ -299,13 +385,13 @@
             pltpu.SMEM((4,), i32),
             pltpu.VMEM((4, 2, 8, N), i32),
             pltpu.VMEM((4, N, 8 * N), bf16),
-            pltpu.VMEM((CHUNK * 2 * ROWS, N), bf16),
-            pltpu.VMEM((2, 2 * N, CHUNK * N), bf16),
-            pltpu.VMEM((4, 2 * N, 2 * N), f32),
-            pltpu.VMEM((4, 2, 4, 4, 8, N), f32),
-            pltpu.VMEM((4, 2, 4, 4, 8, N), f32),
-            dma((5,)), dma((8, 5)), dma((8, 5)), dma((8,)), dma((8,)), dma((7,)), dma((7,)),
-            dma((4, 2, 4)), dma((4, 2, 4)), regular((4,)),
+            pltpu.VMEM((8, CHUNK * 2 * ROWS, N), bf16),
+            pltpu.VMEM((8 * N, CHUNK * N), bf16),
+            pltpu.VMEM((8 * N, 2 * N), f32),
+            pltpu.VMEM((4, 2, 4, 17, N), i32),
+            pltpu.VMEM((4, 2, 4, 17, N), i32),
+            dma((5,)), dma((8, 5)), dma((8, 5)), dma((8, 5)), dma((8, 5)), dma((7,)), dma((7,)),
+            dma((4, 2, 4)), dma((4, 2, 4)), regular((6,)),
         ],
         compiler_params=pltpu.CompilerParams(collective_id=0, has_side_effects=True, vmem_limit_bytes=67043328),
         name="vertex",

time: 52.4 us -> 45.5 us (0.87)
  Pallas kernels: 50.8 us -> 44 us
    pallas_call x1, Pallas kernels: 50.8 us -> 44 us  [body(): pl.pallas_call(kernel, out_shape=jax.ShapeDtypeStruct((4, 8, N), f32), in...]
where the time goes in v3:
time: 45.5 us; the launch traced here: 45.3 us
  Pallas kernels  44 us (97%)
  local copies, waits for them, and re-layouts  1.33 us (3%)
    pallas_call x1, Pallas kernels, body(): pl.pallas_call(kernel, out_shape=jax.ShapeDtypeStruct((4, 8, N), f32), in...  44 us
    reshape x1, local copies, waits for them, and re-layouts, body(): return summed.reshape(4, 2, 4, N).transpose(1, 0, 2, 3)  1.33 us

profile of v3, /device:TPU:1, one launch (start us, length us, event | category | flops | bytes accessed | tf_op | source)
XLA Modules:
  0.0 45.3 jit_solution(580332284407097524)
XLA Ops:
  0.0 44.0 %vertex.1 = f32[4,8,128]{2,1,0:T(8,128)} custom-call(bf16[4,2,128,128]{3,2,1,0:T(8,128)(2,1)} %green.1, s32[4,128]{1,0:T(4,128)} %order.1, s32[4]{0:T(128)} %offset.1), custom_call_target="tpu_custom_call" | custom-call | tf_op jit(solution)/shard_map/vertex/pallas_call | solution.py:377
  44.0 1.3 %copy.6 = f32[4,2,4,128]{3,2,0,1:T(4,128)} copy(f32[4,2,4,128]{3,2,1,0:T(4,128)} %bitcast.4) | data formatting | bytes 32768 | tf_op jit(solution)/shard_map/reshape | solution.py:399

commit v4 on v3

--- a/solution.py
+++ b/solution.py
@@ -11,6 +11,7 @@
 CHUNK = 2 * OWN
 ROWS = 16
 LEVELS = 32766.0
+FIRST = (0, 1, 3, 2)
 CORNERS = [(), (0,), (1,), (2,), (0, 1), (0, 2), (1, 2), (0, 1, 2)]
 ORDERS = [(0, 1, 2), (1, 2, 0), (2, 0, 1), (0, 1, 2), (1, 2, 0)]
 PIECES = range(len(ORDERS))
@@ -167,7 +168,7 @@
     def class_rows(o, h, m, c):
         parts = []
         for b in range(4):
-            start = pl.multiple_of(32 * ((y // 2 + b) % 4) + 16 * (y % 2), 16)
+            start = pl.multiple_of(32 * b + 16 * (y % 2), 16)
             both = held[o, h, m, pl.ds(start, 16), c * N : (c + 1) * N].astype(jnp.float32)
             parts.append(jnp.where(x % 2 == 0, both[0:8], both[8:16]))
         pairs = []
@@ -189,7 +190,7 @@
             wanted = cols[g, t // 4, t % 4 : t % 4 + 1, :]
             select[g, :, t * N : (t + 1) * N] = jnp.where(place == wanted, 1.0, 0.0).astype(jnp.bfloat16)
 
-    order_of = [(zh + 4 - z // 2) % 4 for zh in (0, 1, 3, 2)]
+    order_of = [(zh + 4 - z // 2) % 4 for zh in FIRST]
 
     def pick(g, o, k):
         for t in range(4, 8):
@@ -316,22 +317,24 @@
 
     def finish(k):
         g, base = order_of[k], k * 2 * N
-        for e in range(2):
-            parts = [[], [], [], []]
-            for ti in range(4):
-                for half in range(2):
+        for yh in FIRST:
+            half = yh // 2
+            for e in range(2):
+                parts = []
+                for ti in range(4):
                     r = base + (e * 4 + ti) * ROWS + 8 * half
                     re = total[r : r + 8, 0:N] - total[N + r : N + r + 8, N : 2 * N]
                     im = total[r : r + 8, N : 2 * N] + total[N + r : N + r + 8, 0:N]
-                    parts[2 * half].append(jnp.where(upper, re, pltpu.roll(im, 4, 0)))
-                    parts[2 * half + 1].append(jnp.where(upper, pltpu.roll(re, 4, 0), im))
-            for b in (2, 1, 3, 0):
-                pack(parts[b], mine, (g, e, b))
-                copy = summing(g, e, b)
-                if e or b:
-                    copy.start()
+                    if yh % 2:
+                        parts.append(jnp.where(upper, pltpu.roll(re, 4, 0), im))
+                    else:
+                        parts.append(jnp.where(upper, re, pltpu.roll(im, 4, 0)))
+                b = (yh + 4 - y // 2) % 4
+                pack(parts, mine, (g, e, b))
+                if e:
+                    summing(g, e, b).start()
                 else:
-                    pl.when(g != 0)(copy.start)
+                    pl.when(g + b != 0)(summing(g, e, b).start)
 
     def summing(g, e, b):
         return remote(
@@ -351,7 +354,7 @@
     finish(2)
     finish(3)
     kept = unpack(mine, (0, 0, 0))
-    sums = [(g, e, b) for g in range(4) for e in range(2) for b in range(4)][1:]
+    sums = [(g, e, b) for g in (0, 3, 2, 1) for b in (0, 3, 1, 2) for e in range(2)][1:]
     for at in sums:
         summing(*at).wait_recv()
         kept = [k + u for k, u in zip(kept, unpack(theirs, at))]
@@ -376,7 +379,7 @@
     dma, regular = pltpu.SemaphoreType.DMA, pltpu.SemaphoreType.REGULAR
     summed = pl.pallas_call(
         kernel,
-        out_shape=jax.ShapeDtypeStruct((4, 8, N), f32),
+        out_shape=pltpu.VMEM((4, 8, N), f32),
         in_specs=[pl.BlockSpec(memory_space=pltpu.HBM)] * 3,
         out_specs=pl.BlockSpec(memory_space=pltpu.VMEM),
         scratch_shapes=[
@@ -393,9 +396,9 @@
             dma((5,)), dma((8, 5)), dma((8, 5)), dma((8, 5)), dma((8, 5)), dma((7,)), dma((7,)),
             dma((4, 2, 4)), dma((4, 2, 4)), regular((6,)),
         ],
-        compiler_params=pltpu.CompilerParams(collective_id=0, has_side_effects=True, vmem_limit_bytes=67043328),
+        compiler_params=pltpu.CompilerParams(collective_id=0, has_side_effects=True, vmem_limit_bytes=48 << 20),
         name="vertex",
-    )(green_samples, exchange_index_order, frequency_offset)
+    )(*[pltpu.with_memory_space_constraint(a, pltpu.HBM) for a in (green_samples, exchange_index_order, frequency_offset)])
     return summed.reshape(4, 2, 4, N).transpose(1, 0, 2, 3)
 
 

time: 45.5 us -> 44.2 us (0.971)
  local copies, waits for them, and re-layouts: 1.33 us -> 0.61 us
  Pallas kernels: 44 us -> 43.4 us
    reshape x1, local copies, waits for them, and re-layouts: 1.33 us -> 0.61 us  [body(): return summed.reshape(4, 2, 4, N).transpose(1, 0, 2, 3)]
    pallas_call x1, Pallas kernels: 44 us -> 43.4 us  [body(): pl.pallas_call(kernel, out_shape=pltpu.VMEM((4, 8, N), f32), in_specs=[pl...]
where the time goes in v4:
time: 44.2 us; the launch traced here: 44 us
  Pallas kernels  43.4 us (98%)
  local copies, waits for them, and re-layouts  0.61 us (1%)
    pallas_call x1, Pallas kernels, body(): pl.pallas_call(kernel, out_shape=pltpu.VMEM((4, 8, N), f32), in_specs=[pl...  43.4 us

profile of v4, /device:TPU:1, one launch (start us, length us, event | category | flops | bytes accessed | tf_op | source)
XLA Modules:
  0.0 44.0 jit_solution(8064223378242311237)
XLA Ops:
  0.0 43.4 %vertex.1 = f32[4,8,128]{2,1,0:T(8,128)S(1)} custom-call(bf16[4,2,128,128]{3,2,1,0:T(8,128)(2,1)} %green.1, s32[4,128]{1,0:T(4,128)} %order.1, s32[4]{0:T(128)} %offset.1), custom_call_target="tpu_custom_call" | custom-call | tf_op jit(solution)/shard_map/vertex/pallas_call | solution.py:380
  43.4 0.6 %copy.6 = f32[4,2,4,128]{3,2,0,1:T(4,128)} copy(f32[4,2,4,128]{3,2,1,0:T(4,128)S(1)} %bitcast.4) | data formatting | bytes 32768 | tf_op jit(solution)/shard_map/reshape | solution.py:402
